TPU v7x, 128 devices: a whole 4x4x4 slice. The times are simulated.
128 devices in a mesh: gx: 8 (over y, core), gy: 16 (over z, x).
Axes of the slice: x: 4, y: 4, z: 4, core: 2. Of those that a mesh axis runs over, the one named last changes fastest.
Arguments:
- right_side: float32 [256, 512, 256], P('gx', 'gy'), may hold values from -32 to 32
- phase: int32 [256, 512, 256], P('gx', 'gy'), may hold values from 1 to 3
- table: float32 [4], replicated, may hold values from 0.3 to 3
Outputs:
- solution_field: float32 [256, 512, 256], P('gx', 'gy')
- residual: float32 [256, 512, 256], P('gx', 'gy')
- pre_residual: float32 [256, 512, 256], P('gx', 'gy')
- residual_image: float32 [256, 512, 256], P('gx', 'gy')
Inputs may be any that keep to these rules, and one draw needn't show every extreme that they name: `phase`: labels 1 slag, 2 steel, 3 argon plume; label 0 stands for the lining outside the grid.
All inputs are finite; a program needn't handle non-finite values.
Results may differ from a plain program's by a relative error of at most 0.0003.
Values sent between devices are 32-bit elements; how exact they have to be, the bound alone decides.
No kernel may reach another device: no remote copies, remote signals or barrier semaphores. Data moves between devices by JAX's collectives and lax.ppermute only.
A program may use at most 64 MiB of HBM per device.

v0:
```python
import jax
import jax.numpy as jnp
from jax import lax
from jax.sharding import PartitionSpec as P

ITERS = 2
centre_value = 1.1
half_width = 0.9
ratio_sigma = centre_value / half_width
rho_first = 1.0 / ratio_sigma
rho_second = 1.0 / (2.0 * ratio_sigma - rho_first)
rho_third = 1.0 / (2.0 * ratio_sigma - rho_second)
start_scale = 1.0 / centre_value
keep_first = rho_second * rho_first
push_first = 2.0 * rho_second / half_width
keep_second = rho_third * rho_second
push_second = 2.0 * rho_third / half_width


def extended(block, sides, width):
    for axis, dim in sides:
        count = lax.axis_size(axis)
        forward = [(i, i + 1) for i in range(count - 1)]
        backward = [(target, source) for source, target in forward]
        low = lax.ppermute(
            lax.slice_in_dim(block, block.shape[dim] - width, None, axis=dim), axis, forward
        )
        high = lax.ppermute(lax.slice_in_dim(block, 0, width, axis=dim), axis, backward)
        block = jnp.concatenate([low, block, high], axis=dim)
    return block


def harmonic(left, right):
    return 2.0 * left * right / (left + right)


def coupling_set(sigma_padded):
    centre = sigma_padded[1:-1, 1:-1, 1:-1]
    to_west = harmonic(centre, sigma_padded[:-2, 1:-1, 1:-1])
    to_east = harmonic(centre, sigma_padded[2:, 1:-1, 1:-1])
    to_south = harmonic(centre, sigma_padded[1:-1, :-2, 1:-1])
    to_north = harmonic(centre, sigma_padded[1:-1, 2:, 1:-1])
    to_down = harmonic(centre, sigma_padded[1:-1, 1:-1, :-2])
    to_up = harmonic(centre, sigma_padded[1:-1, 1:-1, 2:])
    diagonal = to_west + to_east + to_south + to_north + to_down + to_up
    return (to_west, to_east, to_south, to_north, to_down, to_up, diagonal)


def lookup(labels, table):
    return jnp.where(
        labels == 1,
        table[1],
        jnp.where(labels == 2, table[2], jnp.where(labels == 3, table[3], table[0])),
    )


def operate_ext(padded_xy, couplings):
    to_west, to_east, to_south, to_north, to_down, to_up, diagonal = couplings
    padded_z = jnp.pad(padded_xy, ((0, 0), (0, 0), (1, 1)))
    centre = padded_xy[1:-1, 1:-1]
    beside = (
        to_west * padded_xy[:-2, 1:-1]
        + to_east * padded_xy[2:, 1:-1]
        + to_south * padded_xy[1:-1, :-2]
        + to_north * padded_xy[1:-1, 2:]
        + to_down * padded_z[1:-1, 1:-1, :-2]
        + to_up * padded_z[1:-1, 1:-1, 2:]
    )
    return diagonal * centre - beside


def local(right_side, phase, table):
    labels_ext = extended(phase, (("gx", 0), ("gy", 1)), 1)
    sigma_ext = lookup(jnp.pad(labels_ext, ((0, 0), (0, 0), (1, 1))), table)
    stored_set = coupling_set(sigma_ext)

    def composite(vector):
        set_zero = tuple((member for member in stored_set))
        diagonal = set_zero[6]

        def image_of(field):
            return operate_ext(extended(field, (("gx", 0), ("gy", 1)), 1), set_zero)

        first = start_scale * (vector / diagonal)
        change = keep_first * first + push_first * ((vector - image_of(first)) / diagonal)
        second = first + change
        change = keep_second * change + push_second * ((vector - image_of(second)) / diagonal)
        third = second + change
        return (third, image_of(third))

    solution_field = jnp.zeros_like(right_side)
    residual = right_side
    pre_residual, residual_image = composite(residual)
    image_dir = jnp.zeros_like(right_side)
    pre_dir = jnp.zeros_like(right_side)
    resid_dir = jnp.zeros_like(right_side)
    direction = jnp.zeros_like(right_side)
    energy_prev = jnp.float32(1.0)
    step_prev = jnp.float32(1.0)
    for iteration in range(ITERS):
        energy_now, curvature = lax.psum(
            (jnp.sum(residual * pre_residual), jnp.sum(residual_image * pre_residual)), ("gx", "gy")
        )
        pre_image, double_image = composite(residual_image)
        if iteration == 0:
            step_size = energy_now / curvature
            image_dir = double_image
            pre_dir = pre_image
            resid_dir = residual_image
            direction = pre_residual
        else:
            momentum = energy_now / energy_prev
            step_size = energy_now / (curvature - momentum * energy_now / step_prev)
            image_dir = double_image + momentum * image_dir
            pre_dir = pre_image + momentum * pre_dir
            resid_dir = residual_image + momentum * resid_dir
            direction = pre_residual + momentum * direction
        solution_field = solution_field + step_size * direction
        residual = residual - step_size * resid_dir
        pre_residual = pre_residual - step_size * pre_dir
        residual_image = residual_image - step_size * image_dir
        energy_prev = energy_now
        step_prev = step_size
    return (solution_field, residual, pre_residual, residual_image)


def solution(mesh):
    placed = (P("gx", "gy", None), P("gx", "gy", None), P())
    return jax.shard_map(
        local,
        mesh=mesh,
        in_specs=placed,
        out_specs=(
            P("gx", "gy", None),
            P("gx", "gy", None),
            P("gx", "gy", None),
            P("gx", "gy", None),
        ),
        check_vma=False,
    )
```

profile of v0, /device:TPU:39, one launch (start us, length us, event | category | flops | bytes accessed | tf_op | source)
XLA Modules:
  0.0 359.8 jit_solution(430377248482108931)
XLA Ops:
  1.4 3.8 %collective-permute-start = (s32[1,32,256]{2,1,0:T(8,128)S(1)}, s32[1,32,256]{2,1,0:T(8,128)S(1)}, u32[]{:S(2)}, u32[]{:S(2)}) collective-permute-start(s32[1,32,256]{2,1,0:T(8,128)S(1)} %get-tuple-element.70), channel_id=1, source_target_pairs={{0,16},{16,32},{32,48},{48,64},{64,80},{80,96},{96,112},{1,17},{17... | collective-permute-start | bytes 98312 | tf_op jit(solution)/shard_map/ppermute | solution.py:25
  10.5 3.5 collective-permute-start.2
  16.5 4.3 %collective-permute-done.3 = s32[34,1,256]{2,1,0:T(1,128)S(1)} collective-permute-done((s32[34,1,256]{2,1,0:T(1,128)S(1)}, s32[34,1,256]{2,1,0:T(1,128)S(1)}, u32[]{:S(2)}, u32[]{:S(2)}) %collective-permute-start.3) | collective-permute-done | bytes 34848 | tf_op jit(solution)/shard_map/ppermute | solution.py:28
  26.5 3.3 collective-permute-start.4
  31.8 3.3 collective-permute-done.5
  37.1 3.4 collective-permute-start.7
  40.5 3.4 collective-permute-done.7
  57.8 3.4 collective-permute-start.11
  61.2 3.4 collective-permute-done.11
  78.6 3.4 collective-permute-start.15
  82.0 3.4 collective-permute-done.15
  86.4 3.3 multiply_reduce_fusion.2
  95.5 3.3 collective-permute-done.17
  100.8 3.5 collective-permute-start.19
  116.2 3.3 collective-permute-done.21
  121.5 3.4 collective-permute-start.23
  124.9 3.4 collective-permute-done.23
  137.0 3.3 collective-permute-done.25
  142.3 3.4 collective-permute-start.27
  145.7 63.7 %all-reduce.11 = (f32[]{:T(128)}, f32[]{:T(128)}) all-reduce(f32[]{:T(128)} %get-tuple-element.7, f32[]{:T(128)} %get-tuple-element.6), channel_id=1, replica_groups=mesh['gx'=8,'gy'=16] {'gx','gy'}, use_global_device_ids=true, to_apply=%region_1.2 | all-reduce | flops 2 | bytes 16 | tf_op jit(solution)/shard_map/psum | solution.py:101
  213.0 6.4 %fusion.125 = (f32[32,32,256]{2,1,0:T(8,128)S(1)}, f32[32,32,256]{2,1,0:T(8,128)S(1)}, f32[32,32,256]{2,1,0:T(8,128)}) fusion(f32[32,32,256]{2,1,0:T(8,128)S(1)} %copy-done.7, f32[32,32,256]{2,1,0:T(8,128)S(1)} %copy-done.4, f32[32,32,256]{2,1,0:T(8,128)S(1)} %copy-done.1, f32[32,32,256]{2,1,0:T(8,128)S(1)} %get-tuple-element.27, ...), kind=kLoop, calls=%fused_computation.275 | loop fusion | flops 7864320 | bytes 13766660 | tf_op jit(solution)/shard_map/mul | solution.py:84
  219.5 4.5 %collective-permute-start.28 = (f32[1,32,256]{2,1,0:T(8,128)S(1)}, f32[1,32,256]{2,1,0:T(8,128)S(1)}, u32[]{:S(2)}, u32[]{:S(2)}) collective-permute-start(f32[1,32,256]{2,1,0:T(8,128)S(1)} %get-tuple-element.55), channel_id=1, source_target_pairs={{0,16},{16,32},{32,48},{48,64},{64,80},{80,96},{96,112},{1,17},{17... | collective-permute-start | bytes 98312 | tf_op jit(solution)/shard_map/ppermute | solution.py:25
  229.3 3.3 collective-permute-start.30
  234.6 4.8 %collective-permute-done.31 = f32[34,1,256]{2,1,0:T(1,128)S(1)} collective-permute-done((f32[34,1,256]{2,1,0:T(1,128)S(1)}, f32[34,1,256]{2,1,0:T(1,128)S(1)}, u32[]{:S(2)}, u32[]{:S(2)}) %collective-permute-start.31) | collective-permute-done | bytes 34848 | tf_op jit(solution)/shard_map/ppermute | solution.py:28
  240.4 3.5 fusion.128
  243.9 3.3 collective-permute-start.32
  254.5 3.6 collective-permute-start.35
  259.3 62.3 %all-reduce.10 = (f32[]{:T(128)}, f32[]{:T(128)}) all-reduce(f32[]{:T(128)} %get-tuple-element.5, f32[]{:T(128)} %get-tuple-element.4), channel_id=1, replica_groups=mesh['gx'=8,'gy'=16] {'gx','gy'}, use_global_device_ids=true, to_apply=%region_5.6 | all-reduce | flops 2 | bytes 16 | tf_op jit(solution)/shard_map/psum | solution.py:101
  328.5 7.3 %multiply_subtract_fusion = (f32[32,32,256]{2,1,0:T(8,128)}, f32[32,32,256]{2,1,0:T(8,128)S(1)}) fusion(f32[32,32,256]{2,1,0:T(8,128)} %copy-done.9, f32[]{:T(128)S(6)} %div.70, f32[]{:T(128)S(6)} %div.72, f32[32,32,256]{2,1,0:T(8,128)} %copy-done.12, f32[]{:T(128)S(6)} %div.66, f32[32,32,256]{2,1,0:T(8,128)} %copy-done.23, f32[32,32,256]{2,1,0:T(8,128)} %copy-done.18, ...), kind=kLoop, calls=%fused_computation.254 | loop fusion | flops 9961472 | bytes 15863820 | tf_op jit(solution)/shard_map/sub | solution.py:120
  335.7 4.2 %collective-permute-start.36 = (f32[1,32,256]{2,1,0:T(8,128)S(1)}, f32[1,32,256]{2,1,0:T(8,128)S(1)}, u32[]{:S(2)}, u32[]{:S(2)}) collective-permute-start(f32[1,32,256]{2,1,0:T(8,128)S(1)} %get-tuple-element.51), channel_id=1, source_target_pairs={{0,16},{16,32},{32,48},{48,64},{64,80},{80,96},{96,112},{1,17},{17... | collective-permute-start | bytes 98312 | tf_op jit(solution)/shard_map/ppermute | solution.py:25
  345.2 3.3 collective-permute-start.38
  356.3 3.5 fusion.5
  (150 shorter events, 113.3 us)
Async XLA Ops:
  1.4 5.7 %collective-permute-start = (s32[1,32,256]{2,1,0:T(8,128)S(1)}, s32[1,32,256]{2,1,0:T(8,128)S(1)}, u32[]{:S(2)}, u32[]{:S(2)}) collective-permute-start(s32[1,32,256]{2,1,0:T(8,128)S(1)} %get-tuple-element.70), channel_id=1, source_target_pairs={{0,16},{16,32},{32,48},{48,64},{64,80},{80,96},{96,112},{1,17},{17... | collective-permute-start | bytes 98312 | tf_op jit(solution)/shard_map/ppermute | solution.py:25
  5.2 5.2 %collective-permute-start.1 = (s32[1,32,256]{2,1,0:T(8,128)S(1)}, s32[1,32,256]{2,1,0:T(8,128)S(1)}, u32[]{:S(2)}, u32[]{:S(2)}) collective-permute-start(s32[1,32,256]{2,1,0:T(8,128)S(1)} %get-tuple-element.69), channel_id=1, source_target_pairs={{16,0},{32,16},{48,32},{64,48},{80,64},{96,80},{112,96},{17,1},{33... | collective-permute-start | bytes 98312 | tf_op jit(solution)/shard_map/ppermute | solution.py:28
  10.5 6.0 %collective-permute-start.2 = (s32[34,1,256]{2,1,0:T(1,128)S(1)}, s32[34,1,256]{2,1,0:T(1,128)S(1)}, u32[]{:S(2)}, u32[]{:S(2)}) collective-permute-start(s32[34,1,256]{2,1,0:T(1,128)S(1)} %get-tuple-element.49), channel_id=1, source_target_pairs={{0,1},{1,2},{2,3},{3,4},{4,5},{5,6},{6,7},{7,8},{8,9},{9,10},{10,1... | collective-permute-start | bytes 104456 | tf_op jit(solution)/shard_map/ppermute | solution.py:25
  13.9 6.8 %collective-permute-start.3 = (s32[34,1,256]{2,1,0:T(1,128)S(1)}, s32[34,1,256]{2,1,0:T(1,128)S(1)}, u32[]{:S(2)}, u32[]{:S(2)}) collective-permute-start(s32[34,1,256]{2,1,0:T(1,128)S(1)} %get-tuple-element.50), channel_id=1, source_target_pairs={{1,0},{2,1},{3,2},{4,3},{5,4},{6,5},{7,6},{8,7},{9,8},{10,9},{11,1... | collective-permute-start | bytes 104456 | tf_op jit(solution)/shard_map/ppermute | solution.py:28
  26.5 5.3 %collective-permute-start.4 = (f32[1,32,256]{2,1,0:T(8,128)S(1)}, f32[1,32,256]{2,1,0:T(8,128)S(1)}, u32[]{:S(2)}, u32[]{:S(2)}) collective-permute-start(f32[1,32,256]{2,1,0:T(8,128)S(1)} %get-tuple-element.67), channel_id=1, source_target_pairs={{0,16},{16,32},{32,48},{48,64},{64,80},{80,96},{96,112},{1,17},{17... | collective-permute-start | bytes 98312 | tf_op jit(solution)/shard_map/ppermute | solution.py:25
  29.9 5.2 %collective-permute-start.5 = (f32[1,32,256]{2,1,0:T(8,128)S(1)}, f32[1,32,256]{2,1,0:T(8,128)S(1)}, u32[]{:S(2)}, u32[]{:S(2)}) collective-permute-start(f32[1,32,256]{2,1,0:T(8,128)S(1)} %get-tuple-element.68), channel_id=1, source_target_pairs={{16,0},{32,16},{48,32},{64,48},{80,64},{96,80},{112,96},{17,1},{33... | collective-permute-start | bytes 98312 | tf_op jit(solution)/shard_map/ppermute | solution.py:28
  35.2 5.3 %collective-permute-start.6 = (f32[34,1,256]{2,1,0:T(1,128)S(1)}, f32[34,1,256]{2,1,0:T(1,128)S(1)}, u32[]{:S(2)}, u32[]{:S(2)}) collective-permute-start(f32[34,1,256]{2,1,0:T(1,128)S(1)} %get-tuple-element.47), channel_id=1, source_target_pairs={{0,1},{1,2},{2,3},{3,4},{4,5},{5,6},{6,7},{7,8},{8,9},{9,10},{10,1... | collective-permute-start | bytes 104456 | tf_op jit(solution)/shard_map/ppermute | solution.py:25
  37.1 6.8 %collective-permute-start.7 = (f32[34,1,256]{2,1,0:T(1,128)S(1)}, f32[34,1,256]{2,1,0:T(1,128)S(1)}, u32[]{:S(2)}, u32[]{:S(2)}) collective-permute-start(f32[34,1,256]{2,1,0:T(1,128)S(1)} %get-tuple-element.48), channel_id=1, source_target_pairs={{1,0},{2,1},{3,2},{4,3},{5,4},{6,5},{7,6},{8,7},{9,8},{10,9},{11,1... | collective-permute-start | bytes 104456 | tf_op jit(solution)/shard_map/ppermute | solution.py:28
  50.6 5.2 %collective-permute-start.9 = (f32[1,32,256]{2,1,0:T(8,128)S(1)}, f32[1,32,256]{2,1,0:T(8,128)S(1)}, u32[]{:S(2)}, u32[]{:S(2)}) collective-permute-start(f32[1,32,256]{2,1,0:T(8,128)S(1)} %get-tuple-element.66), channel_id=1, source_target_pairs={{16,0},{32,16},{48,32},{64,48},{80,64},{96,80},{112,96},{17,1},{33... | collective-permute-start | bytes 98312 | tf_op jit(solution)/shard_map/ppermute | solution.py:28
  55.9 5.3 %collective-permute-start.10 = (f32[34,1,256]{2,1,0:T(1,128)S(1)}, f32[34,1,256]{2,1,0:T(1,128)S(1)}, u32[]{:S(2)}, u32[]{:S(2)}) collective-permute-start(f32[34,1,256]{2,1,0:T(1,128)S(1)} %get-tuple-element.45), channel_id=1, source_target_pairs={{0,1},{1,2},{2,3},{3,4},{4,5},{5,6},{6,7},{7,8},{8,9},{9,10},{10,1... | collective-permute-start | bytes 104456 | tf_op jit(solution)/shard_map/ppermute | solution.py:25
  57.8 6.8 %collective-permute-start.11 = (f32[34,1,256]{2,1,0:T(1,128)S(1)}, f32[34,1,256]{2,1,0:T(1,128)S(1)}, u32[]{:S(2)}, u32[]{:S(2)}) collective-permute-start(f32[34,1,256]{2,1,0:T(1,128)S(1)} %get-tuple-element.46), channel_id=1, source_target_pairs={{1,0},{2,1},{3,2},{4,3},{5,4},{6,5},{7,6},{8,7},{9,8},{10,9},{11,1... | collective-permute-start | bytes 104456 | tf_op jit(solution)/shard_map/ppermute | solution.py:28
  71.4 5.2 %collective-permute-start.13 = (f32[1,32,256]{2,1,0:T(8,128)S(1)}, f32[1,32,256]{2,1,0:T(8,128)S(1)}, u32[]{:S(2)}, u32[]{:S(2)}) collective-permute-start(f32[1,32,256]{2,1,0:T(8,128)S(1)} %get-tuple-element.64), channel_id=1, source_target_pairs={{16,0},{32,16},{48,32},{64,48},{80,64},{96,80},{112,96},{17,1},{33... | collective-permute-start | bytes 98312 | tf_op jit(solution)/shard_map/ppermute | solution.py:28
  76.7 5.3 %collective-permute-start.14 = (f32[34,1,256]{2,1,0:T(1,128)S(1)}, f32[34,1,256]{2,1,0:T(1,128)S(1)}, u32[]{:S(2)}, u32[]{:S(2)}) collective-permute-start(f32[34,1,256]{2,1,0:T(1,128)S(1)} %get-tuple-element.43), channel_id=1, source_target_pairs={{0,1},{1,2},{2,3},{3,4},{4,5},{5,6},{6,7},{7,8},{8,9},{9,10},{10,1... | collective-permute-start | bytes 104456 | tf_op jit(solution)/shard_map/ppermute | solution.py:25
  78.6 6.8 %collective-permute-start.15 = (f32[34,1,256]{2,1,0:T(1,128)S(1)}, f32[34,1,256]{2,1,0:T(1,128)S(1)}, u32[]{:S(2)}, u32[]{:S(2)}) collective-permute-start(f32[34,1,256]{2,1,0:T(1,128)S(1)} %get-tuple-element.44), channel_id=1, source_target_pairs={{1,0},{2,1},{3,2},{4,3},{5,4},{6,5},{7,6},{8,7},{9,8},{10,9},{11,1... | collective-permute-start | bytes 104456 | tf_op jit(solution)/shard_map/ppermute | solution.py:28
  93.6 5.2 %collective-permute-start.17 = (f32[1,32,256]{2,1,0:T(8,128)S(1)}, f32[1,32,256]{2,1,0:T(8,128)S(1)}, u32[]{:S(2)}, u32[]{:S(2)}) collective-permute-start(f32[1,32,256]{2,1,0:T(8,128)S(1)} %get-tuple-element.62), channel_id=1, source_target_pairs={{16,0},{32,16},{48,32},{64,48},{80,64},{96,80},{112,96},{17,1},{33... | collective-permute-start | bytes 98312 | tf_op jit(solution)/shard_map/ppermute | solution.py:28
  98.8 5.5 %collective-permute-start.18 = (f32[34,1,256]{2,1,0:T(1,128)S(1)}, f32[34,1,256]{2,1,0:T(1,128)S(1)}, u32[]{:S(2)}, u32[]{:S(2)}) collective-permute-start(f32[34,1,256]{2,1,0:T(1,128)S(1)} %get-tuple-element.41), channel_id=1, source_target_pairs={{0,1},{1,2},{2,3},{3,4},{4,5},{5,6},{6,7},{7,8},{8,9},{9,10},{10,1... | collective-permute-start | bytes 104456 | tf_op jit(solution)/shard_map/ppermute | solution.py:25
  100.8 6.8 %collective-permute-start.19 = (f32[34,1,256]{2,1,0:T(1,128)S(1)}, f32[34,1,256]{2,1,0:T(1,128)S(1)}, u32[]{:S(2)}, u32[]{:S(2)}) collective-permute-start(f32[34,1,256]{2,1,0:T(1,128)S(1)} %get-tuple-element.42), channel_id=1, source_target_pairs={{1,0},{2,1},{3,2},{4,3},{5,4},{6,5},{7,6},{8,7},{9,8},{10,9},{11,1... | collective-permute-start | bytes 104456 | tf_op jit(solution)/shard_map/ppermute | solution.py:28
  114.3 5.2 %collective-permute-start.21 = (f32[1,32,256]{2,1,0:T(8,128)S(1)}, f32[1,32,256]{2,1,0:T(8,128)S(1)}, u32[]{:S(2)}, u32[]{:S(2)}) collective-permute-start(f32[1,32,256]{2,1,0:T(8,128)S(1)} %get-tuple-element.60), channel_id=1, source_target_pairs={{16,0},{32,16},{48,32},{64,48},{80,64},{96,80},{112,96},{17,1},{33... | collective-permute-start | bytes 98312 | tf_op jit(solution)/shard_map/ppermute | solution.py:28
  119.6 5.3 %collective-permute-start.22 = (f32[34,1,256]{2,1,0:T(1,128)S(1)}, f32[34,1,256]{2,1,0:T(1,128)S(1)}, u32[]{:S(2)}, u32[]{:S(2)}) collective-permute-start(f32[34,1,256]{2,1,0:T(1,128)S(1)} %get-tuple-element.39), channel_id=1, source_target_pairs={{0,1},{1,2},{2,3},{3,4},{4,5},{5,6},{6,7},{7,8},{8,9},{9,10},{10,1... | collective-permute-start | bytes 104456 | tf_op jit(solution)/shard_map/ppermute | solution.py:25
  121.5 6.8 %collective-permute-start.23 = (f32[34,1,256]{2,1,0:T(1,128)S(1)}, f32[34,1,256]{2,1,0:T(1,128)S(1)}, u32[]{:S(2)}, u32[]{:S(2)}) collective-permute-start(f32[34,1,256]{2,1,0:T(1,128)S(1)} %get-tuple-element.40), channel_id=1, source_target_pairs={{1,0},{2,1},{3,2},{4,3},{5,4},{6,5},{7,6},{8,7},{9,8},{10,9},{11,1... | collective-permute-start | bytes 104456 | tf_op jit(solution)/shard_map/ppermute | solution.py:28
  140.4 70.3 %collective-permute-start.26 = (f32[34,1,256]{2,1,0:T(1,128)S(1)}, f32[34,1,256]{2,1,0:T(1,128)S(1)}, u32[]{:S(2)}, u32[]{:S(2)}) collective-permute-start(f32[34,1,256]{2,1,0:T(1,128)S(1)} %get-tuple-element.37), channel_id=1, source_target_pairs={{0,1},{1,2},{2,3},{3,4},{4,5},{5,6},{6,7},{7,8},{8,9},{9,10},{10,1... | collective-permute-start | bytes 104456 | tf_op jit(solution)/shard_map/ppermute | solution.py:25
  142.3 68.4 %collective-permute-start.27 = (f32[34,1,256]{2,1,0:T(1,128)S(1)}, f32[34,1,256]{2,1,0:T(1,128)S(1)}, u32[]{:S(2)}, u32[]{:S(2)}) collective-permute-start(f32[34,1,256]{2,1,0:T(1,128)S(1)} %get-tuple-element.38), channel_id=1, source_target_pairs={{1,0},{2,1},{3,2},{4,3},{5,4},{6,5},{7,6},{8,7},{9,8},{10,9},{11,1... | collective-permute-start | bytes 104456 | tf_op jit(solution)/shard_map/ppermute | solution.py:28
  219.5 6.4 %collective-permute-start.28 = (f32[1,32,256]{2,1,0:T(8,128)S(1)}, f32[1,32,256]{2,1,0:T(8,128)S(1)}, u32[]{:S(2)}, u32[]{:S(2)}) collective-permute-start(f32[1,32,256]{2,1,0:T(8,128)S(1)} %get-tuple-element.55), channel_id=1, source_target_pairs={{0,16},{16,32},{32,48},{48,64},{64,80},{80,96},{96,112},{1,17},{17... | collective-permute-start | bytes 98312 | tf_op jit(solution)/shard_map/ppermute | solution.py:25
  229.3 5.3 %collective-permute-start.30 = (f32[34,1,256]{2,1,0:T(1,128)S(1)}, f32[34,1,256]{2,1,0:T(1,128)S(1)}, u32[]{:S(2)}, u32[]{:S(2)}) collective-permute-start(f32[34,1,256]{2,1,0:T(1,128)S(1)} %get-tuple-element.35), channel_id=1, source_target_pairs={{0,1},{1,2},{2,3},{3,4},{4,5},{5,6},{6,7},{7,8},{8,9},{9,10},{10,1... | collective-permute-start | bytes 104456 | tf_op jit(solution)/shard_map/ppermute | solution.py:25
  232.6 6.8 %collective-permute-start.31 = (f32[34,1,256]{2,1,0:T(1,128)S(1)}, f32[34,1,256]{2,1,0:T(1,128)S(1)}, u32[]{:S(2)}, u32[]{:S(2)}) collective-permute-start(f32[34,1,256]{2,1,0:T(1,128)S(1)} %get-tuple-element.36), channel_id=1, source_target_pairs={{1,0},{2,1},{3,2},{4,3},{5,4},{6,5},{7,6},{8,7},{9,8},{10,9},{11,1... | collective-permute-start | bytes 104456 | tf_op jit(solution)/shard_map/ppermute | solution.py:28
  243.9 5.3 %collective-permute-start.32 = (f32[1,32,256]{2,1,0:T(8,128)S(1)}, f32[1,32,256]{2,1,0:T(8,128)S(1)}, u32[]{:S(2)}, u32[]{:S(2)}) collective-permute-start(f32[1,32,256]{2,1,0:T(8,128)S(1)} %get-tuple-element.53), channel_id=1, source_target_pairs={{0,16},{16,32},{32,48},{48,64},{64,80},{80,96},{96,112},{1,17},{17... | collective-permute-start | bytes 98312 | tf_op jit(solution)/shard_map/ppermute | solution.py:25
  252.6 73.5 %collective-permute-start.34 = (f32[34,1,256]{2,1,0:T(1,128)S(1)}, f32[34,1,256]{2,1,0:T(1,128)S(1)}, u32[]{:S(2)}, u32[]{:S(2)}) collective-permute-start(f32[34,1,256]{2,1,0:T(1,128)S(1)} %get-tuple-element.33), channel_id=1, source_target_pairs={{0,1},{1,2},{2,3},{3,4},{4,5},{5,6},{6,7},{7,8},{8,9},{9,10},{10,1... | collective-permute-start | bytes 104456 | tf_op jit(solution)/shard_map/ppermute | solution.py:25
  254.5 71.6 %collective-permute-start.35 = (f32[34,1,256]{2,1,0:T(1,128)S(1)}, f32[34,1,256]{2,1,0:T(1,128)S(1)}, u32[]{:S(2)}, u32[]{:S(2)}) collective-permute-start(f32[34,1,256]{2,1,0:T(1,128)S(1)} %get-tuple-element.34), channel_id=1, source_target_pairs={{1,0},{2,1},{3,2},{4,3},{5,4},{6,5},{7,6},{8,7},{9,8},{10,9},{11,1... | collective-permute-start | bytes 104456 | tf_op jit(solution)/shard_map/ppermute | solution.py:28
  335.7 6.1 %collective-permute-start.36 = (f32[1,32,256]{2,1,0:T(8,128)S(1)}, f32[1,32,256]{2,1,0:T(8,128)S(1)}, u32[]{:S(2)}, u32[]{:S(2)}) collective-permute-start(f32[1,32,256]{2,1,0:T(8,128)S(1)} %get-tuple-element.51), channel_id=1, source_target_pairs={{0,16},{16,32},{32,48},{48,64},{64,80},{80,96},{96,112},{1,17},{17... | collective-permute-start | bytes 98312 | tf_op jit(solution)/shard_map/ppermute | solution.py:25
  339.9 5.2 %collective-permute-start.37 = (f32[1,32,256]{2,1,0:T(8,128)S(1)}, f32[1,32,256]{2,1,0:T(8,128)S(1)}, u32[]{:S(2)}, u32[]{:S(2)}) collective-permute-start(f32[1,32,256]{2,1,0:T(8,128)S(1)} %get-tuple-element.52), channel_id=1, source_target_pairs={{16,0},{32,16},{48,32},{64,48},{80,64},{96,80},{112,96},{17,1},{33... | collective-permute-start | bytes 98312 | tf_op jit(solution)/shard_map/ppermute | solution.py:28
  345.2 7.3 %collective-permute-start.38 = (f32[34,1,256]{2,1,0:T(1,128)S(1)}, f32[34,1,256]{2,1,0:T(1,128)S(1)}, u32[]{:S(2)}, u32[]{:S(2)}) collective-permute-start(f32[34,1,256]{2,1,0:T(1,128)S(1)} %get-tuple-element.31), channel_id=1, source_target_pairs={{0,1},{1,2},{2,3},{3,4},{4,5},{5,6},{6,7},{7,8},{8,9},{9,10},{10,1... | collective-permute-start | bytes 104456 | tf_op jit(solution)/shard_map/ppermute | solution.py:25
  348.5 6.8 %collective-permute-start.39 = (f32[34,1,256]{2,1,0:T(1,128)S(1)}, f32[34,1,256]{2,1,0:T(1,128)S(1)}, u32[]{:S(2)}, u32[]{:S(2)}) collective-permute-start(f32[34,1,256]{2,1,0:T(1,128)S(1)} %get-tuple-element.32), channel_id=1, source_target_pairs={{1,0},{2,1},{3,2},{4,3},{5,4},{6,5},{7,6},{8,7},{9,8},{10,9},{11,1... | collective-permute-start | bytes 104456 | tf_op jit(solution)/shard_map/ppermute | solution.py:28
  (34 other events, 686.7 us)
where the time goes:
time: 361 us; the launch traced here: 360 us
  blocking collectives  126 us (35%)
  starting transfers between devices  107 us (30%)
  waiting for transfers between devices  60.4 us (17%)
  other arithmetic  56.1 us (16%)
  between operations  7.42 us (2%)
    psum x2, blocking collectives, local(): lax.psum((jnp.sum(residual * pre_residual), jnp.sum(residual_image * pre_...  126 us
    ppermute x20, waiting for transfers between devices, extended(): lax.ppermute(lax.slice_in_dim(block, 0, width, axis=dim), axis, backward)  60.4 us
    ppermute x20, starting transfers between devices, extended(): lax.ppermute(lax.slice_in_dim(block, block.shape[dim] - width, None, axis...  57.9 us
    ppermute x20, starting transfers between devices, extended(): lax.ppermute(lax.slice_in_dim(block, 0, width, axis=dim), axis, backward)  49 us
    concatenate x10, other arithmetic, extended(): block = jnp.concatenate([low, block, high], axis=dim)  11.3 us
    mul x3, other arithmetic, composite(): first = start_scale * (vector / diagonal)  9.5 us
    add x3, other arithmetic, composite(): second = first + change  8.92 us
    sub x1, other arithmetic, local(): pre_residual = pre_residual - step_size * pre_dir  7.26 us
  transfers between devices with their start and end apart: 40, of which 18 were waited for; matrix products, arithmetic and copies ran while one was open for 1% of the time, Pallas kernels for 0%

commit v1 on v0

--- a/solution.py
+++ b/solution.py
@@ -2,6 +2,7 @@
 import jax.numpy as jnp
 from jax import lax
 from jax.sharding import PartitionSpec as P
+from jax.lax import psum
 
 ITERS = 2
 centre_value = 1.1
@@ -98,8 +99,9 @@
     energy_prev = jnp.float32(1.0)
     step_prev = jnp.float32(1.0)
     for iteration in range(ITERS):
-        energy_now, curvature = lax.psum(
-            (jnp.sum(residual * pre_residual), jnp.sum(residual_image * pre_residual)), ("gx", "gy")
+        energy_now, curvature = psum(
+            psum((jnp.sum(residual * pre_residual), jnp.sum(residual_image * pre_residual)), "gy"),
+            "gx",
         )
         pre_image, double_image = composite(residual_image)
         if iteration == 0:

time: 361 us -> 322 us (0.89)
  blocking collectives: 126 us -> 85.9 us
    psum x2 -> x4, blocking collectives: 126 us -> 85.9 us  [the longest x2 48.6 us: local(): psum((jnp.sum(residual * pre_residual), jnp.sum(residual_image * pre_resi...]
  transfers between devices with their start and end apart: 40 -> 40, of which waited for: 18 -> 18; matrix products, arithmetic and copies ran while one was open for 1% -> 2% of each run, Pallas kernels for 0% -> 0%
where the time goes in v1:
time: 322 us; the launch traced here: 321 us
  starting transfers between devices  108 us (34%)
  blocking collectives  85.9 us (27%)
  waiting for transfers between devices  59.8 us (19%)
  other arithmetic  56.4 us (18%)
  between operations  7.72 us (2%)
    ppermute x20, waiting for transfers between devices, extended(): lax.ppermute(lax.slice_in_dim(block, 0, width, axis=dim), axis, backward)  59.8 us
    ppermute x20, starting transfers between devices, extended(): lax.ppermute(lax.slice_in_dim(block, block.shape[dim] - width, None, axis...  58.3 us
    ppermute x20, starting transfers between devices, extended(): lax.ppermute(lax.slice_in_dim(block, 0, width, axis=dim), axis, backward)  49.4 us
    psum x2, blocking collectives, local(): psum((jnp.sum(residual * pre_residual), jnp.sum(residual_image * pre_resi...  48.6 us
    psum x2, blocking collectives, local(): psum(psum((jnp.sum(residual * pre_residual), jnp.sum(residual_image * pre...  37.4 us
    concatenate x10, other arithmetic, extended(): block = jnp.concatenate([low, block, high], axis=dim)  11.3 us
    mul x3, other arithmetic, composite(): first = start_scale * (vector / diagonal)  9.67 us
    add x3, other arithmetic, composite(): second = first + change  8.9 us
  transfers between devices with their start and end apart: 40, of which 18 were waited for; matrix products, arithmetic and copies ran while one was open for 2% of the time, Pallas kernels for 0%

profile of v1, /device:TPU:39, one launch (start us, length us, event | category | flops | bytes accessed | tf_op | source)
XLA Modules:
  0.0 320.5 jit_solution(18513038543344012)
XLA Ops:
  1.4 3.8 %collective-permute-start = (s32[1,32,256]{2,1,0:T(8,128)S(1)}, s32[1,32,256]{2,1,0:T(8,128)S(1)}, u32[]{:S(2)}, u32[]{:S(2)}) collective-permute-start(s32[1,32,256]{2,1,0:T(8,128)S(1)} %get-tuple-element.74), channel_id=1, source_target_pairs={{0,16},{16,32},{32,48},{48,64},{64,80},{80,96},{96,112},{1,17},{17... | collective-permute-start | bytes 98312 | tf_op jit(solution)/shard_map/ppermute | solution.py:26
  10.5 3.5 %collective-permute-start.2 = (s32[34,1,256]{2,1,0:T(1,128)S(1)}, s32[34,1,256]{2,1,0:T(1,128)S(1)}, u32[]{:S(2)}, u32[]{:S(2)}) collective-permute-start(s32[34,1,256]{2,1,0:T(1,128)S(1)} %get-tuple-element.53), channel_id=1, source_target_pairs={{0,1},{1,2},{2,3},{3,4},{4,5},{5,6},{6,7},{7,8},{8,9},{9,10},{10,1... | collective-permute-start | bytes 104456 | tf_op jit(solution)/shard_map/ppermute | solution.py:26
  16.5 4.3 %collective-permute-done.3 = s32[34,1,256]{2,1,0:T(1,128)S(1)} collective-permute-done((s32[34,1,256]{2,1,0:T(1,128)S(1)}, s32[34,1,256]{2,1,0:T(1,128)S(1)}, u32[]{:S(2)}, u32[]{:S(2)}) %collective-permute-start.3) | collective-permute-done | bytes 34848 | tf_op jit(solution)/shard_map/ppermute | solution.py:29
  26.5 3.3 %collective-permute-start.4 = (f32[1,32,256]{2,1,0:T(8,128)S(1)}, f32[1,32,256]{2,1,0:T(8,128)S(1)}, u32[]{:S(2)}, u32[]{:S(2)}) collective-permute-start(f32[1,32,256]{2,1,0:T(8,128)S(1)} %get-tuple-element.71), channel_id=1, source_target_pairs={{0,16},{16,32},{32,48},{48,64},{64,80},{80,96},{96,112},{1,17},{17... | collective-permute-start | bytes 98312 | tf_op jit(solution)/shard_map/ppermute | solution.py:26
  31.8 3.3 %collective-permute-done.5 = f32[1,32,256]{2,1,0:T(8,128)S(1)} collective-permute-done((f32[1,32,256]{2,1,0:T(8,128)S(1)}, f32[1,32,256]{2,1,0:T(8,128)S(1)}, u32[]{:S(2)}, u32[]{:S(2)}) %collective-permute-start.5) | collective-permute-done | bytes 32800 | tf_op jit(solution)/shard_map/ppermute | solution.py:29
  37.1 3.4 %collective-permute-start.7 = (f32[34,1,256]{2,1,0:T(1,128)S(1)}, f32[34,1,256]{2,1,0:T(1,128)S(1)}, u32[]{:S(2)}, u32[]{:S(2)}) collective-permute-start(f32[34,1,256]{2,1,0:T(1,128)S(1)} %get-tuple-element.52), channel_id=1, source_target_pairs={{1,0},{2,1},{3,2},{4,3},{5,4},{6,5},{7,6},{8,7},{9,8},{10,9},{11,1... | collective-permute-start | bytes 104456 | tf_op jit(solution)/shard_map/ppermute | solution.py:29
  40.5 3.4 %collective-permute-done.7 = f32[34,1,256]{2,1,0:T(1,128)S(1)} collective-permute-done((f32[34,1,256]{2,1,0:T(1,128)S(1)}, f32[34,1,256]{2,1,0:T(1,128)S(1)}, u32[]{:S(2)}, u32[]{:S(2)}) %collective-permute-start.7) | collective-permute-done | bytes 34848 | tf_op jit(solution)/shard_map/ppermute | solution.py:29
  57.8 3.4 %collective-permute-start.11 = (f32[34,1,256]{2,1,0:T(1,128)S(1)}, f32[34,1,256]{2,1,0:T(1,128)S(1)}, u32[]{:S(2)}, u32[]{:S(2)}) collective-permute-start(f32[34,1,256]{2,1,0:T(1,128)S(1)} %get-tuple-element.50), channel_id=1, source_target_pairs={{1,0},{2,1},{3,2},{4,3},{5,4},{6,5},{7,6},{8,7},{9,8},{10,9},{11,1... | collective-permute-start | bytes 104456 | tf_op jit(solution)/shard_map/ppermute | solution.py:29
  61.2 3.4 %collective-permute-done.11 = f32[34,1,256]{2,1,0:T(1,128)S(1)} collective-permute-done((f32[34,1,256]{2,1,0:T(1,128)S(1)}, f32[34,1,256]{2,1,0:T(1,128)S(1)}, u32[]{:S(2)}, u32[]{:S(2)}) %collective-permute-start.11) | collective-permute-done | bytes 34848 | tf_op jit(solution)/shard_map/ppermute | solution.py:29
  78.6 3.4 %collective-permute-start.15 = (f32[34,1,256]{2,1,0:T(1,128)S(1)}, f32[34,1,256]{2,1,0:T(1,128)S(1)}, u32[]{:S(2)}, u32[]{:S(2)}) collective-permute-start(f32[34,1,256]{2,1,0:T(1,128)S(1)} %get-tuple-element.48), channel_id=1, source_target_pairs={{1,0},{2,1},{3,2},{4,3},{5,4},{6,5},{7,6},{8,7},{9,8},{10,9},{11,1... | collective-permute-start | bytes 104456 | tf_op jit(solution)/shard_map/ppermute | solution.py:29
  82.0 3.4 %collective-permute-done.15 = f32[34,1,256]{2,1,0:T(1,128)S(1)} collective-permute-done((f32[34,1,256]{2,1,0:T(1,128)S(1)}, f32[34,1,256]{2,1,0:T(1,128)S(1)}, u32[]{:S(2)}, u32[]{:S(2)}) %collective-permute-start.15) | collective-permute-done | bytes 34848 | tf_op jit(solution)/shard_map/ppermute | solution.py:29
  95.5 3.3 %collective-permute-done.17 = f32[1,32,256]{2,1,0:T(8,128)S(1)} collective-permute-done((f32[1,32,256]{2,1,0:T(8,128)S(1)}, f32[1,32,256]{2,1,0:T(8,128)S(1)}, u32[]{:S(2)}, u32[]{:S(2)}) %collective-permute-start.17) | collective-permute-done | bytes 32800 | tf_op jit(solution)/shard_map/ppermute | solution.py:29
  100.7 3.5 %collective-permute-start.19 = (f32[34,1,256]{2,1,0:T(1,128)S(1)}, f32[34,1,256]{2,1,0:T(1,128)S(1)}, u32[]{:S(2)}, u32[]{:S(2)}) collective-permute-start(f32[34,1,256]{2,1,0:T(1,128)S(1)} %get-tuple-element.46), channel_id=1, source_target_pairs={{1,0},{2,1},{3,2},{4,3},{5,4},{6,5},{7,6},{8,7},{9,8},{10,9},{11,1... | collective-permute-start | bytes 104456 | tf_op jit(solution)/shard_map/ppermute | solution.py:29
  116.2 3.3 %collective-permute-done.21 = f32[1,32,256]{2,1,0:T(8,128)S(1)} collective-permute-done((f32[1,32,256]{2,1,0:T(8,128)S(1)}, f32[1,32,256]{2,1,0:T(8,128)S(1)}, u32[]{:S(2)}, u32[]{:S(2)}) %collective-permute-start.21) | collective-permute-done | bytes 32800 | tf_op jit(solution)/shard_map/ppermute | solution.py:29
  121.5 3.4 %collective-permute-start.23 = (f32[34,1,256]{2,1,0:T(1,128)S(1)}, f32[34,1,256]{2,1,0:T(1,128)S(1)}, u32[]{:S(2)}, u32[]{:S(2)}) collective-permute-start(f32[34,1,256]{2,1,0:T(1,128)S(1)} %get-tuple-element.44), channel_id=1, source_target_pairs={{1,0},{2,1},{3,2},{4,3},{5,4},{6,5},{7,6},{8,7},{9,8},{10,9},{11,1... | collective-permute-start | bytes 104456 | tf_op jit(solution)/shard_map/ppermute | solution.py:29
  124.8 3.4 %collective-permute-done.23 = f32[34,1,256]{2,1,0:T(1,128)S(1)} collective-permute-done((f32[34,1,256]{2,1,0:T(1,128)S(1)}, f32[34,1,256]{2,1,0:T(1,128)S(1)}, u32[]{:S(2)}, u32[]{:S(2)}) %collective-permute-start.23) | collective-permute-done | bytes 34848 | tf_op jit(solution)/shard_map/ppermute | solution.py:29
  137.0 3.3 %collective-permute-done.25 = f32[1,32,256]{2,1,0:T(8,128)S(1)} collective-permute-done((f32[1,32,256]{2,1,0:T(8,128)S(1)}, f32[1,32,256]{2,1,0:T(8,128)S(1)}, u32[]{:S(2)}, u32[]{:S(2)}) %collective-permute-start.25) | collective-permute-done | bytes 32800 | tf_op jit(solution)/shard_map/ppermute | solution.py:29
  142.3 3.4 %collective-permute-start.27 = (f32[34,1,256]{2,1,0:T(1,128)S(1)}, f32[34,1,256]{2,1,0:T(1,128)S(1)}, u32[]{:S(2)}, u32[]{:S(2)}) collective-permute-start(f32[34,1,256]{2,1,0:T(1,128)S(1)} %get-tuple-element.42), channel_id=1, source_target_pairs={{1,0},{2,1},{3,2},{4,3},{5,4},{6,5},{7,6},{8,7},{9,8},{10,9},{11,1... | collective-permute-start | bytes 104456 | tf_op jit(solution)/shard_map/ppermute | solution.py:29
  145.7 24.2 %all-reduce.11 = (f32[]{:T(128)}, f32[]{:T(128)}) all-reduce(f32[]{:T(128)} %get-tuple-element.7, f32[]{:T(128)} %get-tuple-element.6), channel_id=1, replica_groups=mesh['gx'=8,'gy'=16] {'gy'}, use_global_device_ids=true, to_apply=%region_1.2 | all-reduce | flops 2 | bytes 16 | tf_op jit(solution)/shard_map/psum | solution.py:103
  169.9 19.0 %all-reduce.13 = (f32[]{:T(128)}, f32[]{:T(128)}) all-reduce(f32[]{:T(128)} %get-tuple-element.10, f32[]{:T(128)} %get-tuple-element.11), channel_id=1, replica_groups=mesh['gx'=8,'gy'=16] {'gx'}, use_global_device_ids=true, to_apply=%region_2.3 | all-reduce | flops 2 | bytes 16 | tf_op jit(solution)/shard_map/psum | solution.py:102
  192.6 6.6 %fusion.125 = (f32[32,32,256]{2,1,0:T(8,128)S(1)}, f32[32,32,256]{2,1,0:T(8,128)S(1)}, f32[32,32,256]{2,1,0:T(8,128)}) fusion(f32[32,32,256]{2,1,0:T(8,128)S(1)} %copy-done.7, f32[32,32,256]{2,1,0:T(8,128)S(1)} %copy-done.4, f32[32,32,256]{2,1,0:T(8,128)S(1)} %copy-done.1, f32[32,32,256]{2,1,0:T(8,128)S(1)} %get-tuple-element.31, ...), kind=kLoop, calls=%fused_computation.275 | loop fusion | flops 7864320 | bytes 13766660 | tf_op jit(solution)/shard_map/mul | solution.py:85
  206.5 5.7 %collective-permute-start.30 = (f32[34,1,256]{2,1,0:T(1,128)S(1)}, f32[34,1,256]{2,1,0:T(1,128)S(1)}, u32[]{:S(2)}, u32[]{:S(2)}) collective-permute-start(f32[34,1,256]{2,1,0:T(1,128)S(1)} %get-tuple-element.39), channel_id=1, source_target_pairs={{0,1},{1,2},{2,3},{3,4},{4,5},{5,6},{6,7},{7,8},{8,9},{9,10},{10,1... | collective-permute-start | bytes 104456 | tf_op jit(solution)/shard_map/ppermute | solution.py:26
  214.2 4.9 %collective-permute-done.31 = f32[34,1,256]{2,1,0:T(1,128)S(1)} collective-permute-done((f32[34,1,256]{2,1,0:T(1,128)S(1)}, f32[34,1,256]{2,1,0:T(1,128)S(1)}, u32[]{:S(2)}, u32[]{:S(2)}) %collective-permute-start.31) | collective-permute-done | bytes 34848 | tf_op jit(solution)/shard_map/ppermute | solution.py:29
  220.0 3.5 %fusion.128 = (f32[32,32,256]{2,1,0:T(8,128)S(1)}, f32[32,32,256]{2,1,0:T(8,128)}) fusion(f32[32,32,256]{2,1,0:T(8,128)S(1)} %get-tuple-element.20, f32[32,32,256]{2,1,0:T(8,128)S(1)} %get-tuple-element.21, f32[32,32,256]{2,1,0:T(8,128)S(1)} %copy-done.7, f32[34,34,258]{2,1,0:T(8,128)S(1)} %select_maximum_fusion.8, f32[32,32,256]{2,1,0:T(8,128)S(1)} %copy-done.4, ...), kind=kLoop, calls=%fused_computation.307 | loop fusion | flops 8650752 | bytes 12718080 | tf_op jit(solution)/shard_map/add | solution.py:87
  223.5 3.3 %collective-permute-start.32 = (f32[1,32,256]{2,1,0:T(8,128)S(1)}, f32[1,32,256]{2,1,0:T(8,128)S(1)}, u32[]{:S(2)}, u32[]{:S(2)}) collective-permute-start(f32[1,32,256]{2,1,0:T(8,128)S(1)} %get-tuple-element.57), channel_id=1, source_target_pairs={{0,16},{16,32},{32,48},{48,64},{64,80},{80,96},{96,112},{1,17},{17... | collective-permute-start | bytes 98312 | tf_op jit(solution)/shard_map/ppermute | solution.py:26
  228.8 3.3 %collective-permute-done.33 = f32[1,32,256]{2,1,0:T(8,128)S(1)} collective-permute-done((f32[1,32,256]{2,1,0:T(8,128)S(1)}, f32[1,32,256]{2,1,0:T(8,128)S(1)}, u32[]{:S(2)}, u32[]{:S(2)}) %collective-permute-start.33) | collective-permute-done | bytes 32800 | tf_op jit(solution)/shard_map/ppermute | solution.py:29
  234.1 3.4 %collective-permute-start.35 = (f32[34,1,256]{2,1,0:T(1,128)S(1)}, f32[34,1,256]{2,1,0:T(1,128)S(1)}, u32[]{:S(2)}, u32[]{:S(2)}) collective-permute-start(f32[34,1,256]{2,1,0:T(1,128)S(1)} %get-tuple-element.38), channel_id=1, source_target_pairs={{1,0},{2,1},{3,2},{4,3},{5,4},{6,5},{7,6},{8,7},{9,8},{10,9},{11,1... | collective-permute-start | bytes 104456 | tf_op jit(solution)/shard_map/ppermute | solution.py:29
  238.7 24.4 %all-reduce.10 = (f32[]{:T(128)}, f32[]{:T(128)}) all-reduce(f32[]{:T(128)} %get-tuple-element.5, f32[]{:T(128)} %get-tuple-element.4), channel_id=1, replica_groups=mesh['gx'=8,'gy'=16] {'gy'}, use_global_device_ids=true, to_apply=%region_7.8 | all-reduce | flops 2 | bytes 16 | tf_op jit(solution)/shard_map/psum | solution.py:103
  263.1 18.4 %all-reduce.12 = (f32[]{:T(128)}, f32[]{:T(128)}) all-reduce(f32[]{:T(128)} %get-tuple-element.8, f32[]{:T(128)} %get-tuple-element.9), channel_id=1, replica_groups=mesh['gx'=8,'gy'=16] {'gx'}, use_global_device_ids=true, to_apply=%region_8.9 | all-reduce | flops 2 | bytes 16 | tf_op jit(solution)/shard_map/psum | solution.py:102
  288.5 7.4 %multiply_subtract_fusion = (f32[32,32,256]{2,1,0:T(8,128)}, f32[32,32,256]{2,1,0:T(8,128)S(1)}) fusion(f32[32,32,256]{2,1,0:T(8,128)} %copy-done.9, f32[]{:T(128)S(6)} %div.70, f32[]{:T(128)S(6)} %div.72, f32[32,32,256]{2,1,0:T(8,128)} %copy-done.12, f32[]{:T(128)S(6)} %div.66, f32[32,32,256]{2,1,0:T(8,128)} %copy-done.23, f32[32,32,256]{2,1,0:T(8,128)} %copy-done.18, ...), kind=kLoop, calls=%fused_computation.254 | loop fusion | flops 9961472 | bytes 15863820 | tf_op jit(solution)/shard_map/sub | solution.py:122
  303.5 5.7 %collective-permute-start.38 = (f32[34,1,256]{2,1,0:T(1,128)S(1)}, f32[34,1,256]{2,1,0:T(1,128)S(1)}, u32[]{:S(2)}, u32[]{:S(2)}) collective-permute-start(f32[34,1,256]{2,1,0:T(1,128)S(1)} %get-tuple-element.35), channel_id=1, source_target_pairs={{0,1},{1,2},{2,3},{3,4},{4,5},{5,6},{6,7},{7,8},{8,9},{9,10},{10,1... | collective-permute-start | bytes 104456 | tf_op jit(solution)/shard_map/ppermute | solution.py:26
  317.0 3.5 %fusion.5 = f32[32,32,256]{2,1,0:T(8,128)} fusion(f32[32,32,256]{2,1,0:T(8,128)S(1)} %copy-done.19, f32[32,32,256]{2,1,0:T(8,128)S(1)} %copy-done.8, f32[34,34,258]{2,1,0:T(8,128)S(1)} %select_maximum_fusion, f32[32,32,256]{2,1,0:T(8,128)S(1)} %copy-done.5, f32[32,32,256]{2,1,0:T(8,128)S(1)} %copy-done.2, f32[34,1,256]{2,1,0:T(1,128)S(1)} %collective-permute-done.39, ...), kind=kLoop, calls=%fused_computation.49 | loop fusion | flops 7864320 | bytes 12718088 | tf_op jit(solution)/shard_map/sub | solution.py:123
  (152 shorter events, 117.5 us)
Async XLA Ops:
  1.4 5.7 %collective-permute-start = (s32[1,32,256]{2,1,0:T(8,128)S(1)}, s32[1,32,256]{2,1,0:T(8,128)S(1)}, u32[]{:S(2)}, u32[]{:S(2)}) collective-permute-start(s32[1,32,256]{2,1,0:T(8,128)S(1)} %get-tuple-element.74), channel_id=1, source_target_pairs={{0,16},{16,32},{32,48},{48,64},{64,80},{80,96},{96,112},{1,17},{17... | collective-permute-start | bytes 98312 | tf_op jit(solution)/shard_map/ppermute | solution.py:26
  5.2 5.2 %collective-permute-start.1 = (s32[1,32,256]{2,1,0:T(8,128)S(1)}, s32[1,32,256]{2,1,0:T(8,128)S(1)}, u32[]{:S(2)}, u32[]{:S(2)}) collective-permute-start(s32[1,32,256]{2,1,0:T(8,128)S(1)} %get-tuple-element.73), channel_id=1, source_target_pairs={{16,0},{32,16},{48,32},{64,48},{80,64},{96,80},{112,96},{17,1},{33... | collective-permute-start | bytes 98312 | tf_op jit(solution)/shard_map/ppermute | solution.py:29
  10.5 6.0 %collective-permute-start.2 = (s32[34,1,256]{2,1,0:T(1,128)S(1)}, s32[34,1,256]{2,1,0:T(1,128)S(1)}, u32[]{:S(2)}, u32[]{:S(2)}) collective-permute-start(s32[34,1,256]{2,1,0:T(1,128)S(1)} %get-tuple-element.53), channel_id=1, source_target_pairs={{0,1},{1,2},{2,3},{3,4},{4,5},{5,6},{6,7},{7,8},{8,9},{9,10},{10,1... | collective-permute-start | bytes 104456 | tf_op jit(solution)/shard_map/ppermute | solution.py:26
  13.9 6.8 %collective-permute-start.3 = (s32[34,1,256]{2,1,0:T(1,128)S(1)}, s32[34,1,256]{2,1,0:T(1,128)S(1)}, u32[]{:S(2)}, u32[]{:S(2)}) collective-permute-start(s32[34,1,256]{2,1,0:T(1,128)S(1)} %get-tuple-element.54), channel_id=1, source_target_pairs={{1,0},{2,1},{3,2},{4,3},{5,4},{6,5},{7,6},{8,7},{9,8},{10,9},{11,1... | collective-permute-start | bytes 104456 | tf_op jit(solution)/shard_map/ppermute | solution.py:29
  26.5 5.3 %collective-permute-start.4 = (f32[1,32,256]{2,1,0:T(8,128)S(1)}, f32[1,32,256]{2,1,0:T(8,128)S(1)}, u32[]{:S(2)}, u32[]{:S(2)}) collective-permute-start(f32[1,32,256]{2,1,0:T(8,128)S(1)} %get-tuple-element.71), channel_id=1, source_target_pairs={{0,16},{16,32},{32,48},{48,64},{64,80},{80,96},{96,112},{1,17},{17... | collective-permute-start | bytes 98312 | tf_op jit(solution)/shard_map/ppermute | solution.py:26
  29.9 5.2 %collective-permute-start.5 = (f32[1,32,256]{2,1,0:T(8,128)S(1)}, f32[1,32,256]{2,1,0:T(8,128)S(1)}, u32[]{:S(2)}, u32[]{:S(2)}) collective-permute-start(f32[1,32,256]{2,1,0:T(8,128)S(1)} %get-tuple-element.72), channel_id=1, source_target_pairs={{16,0},{32,16},{48,32},{64,48},{80,64},{96,80},{112,96},{17,1},{33... | collective-permute-start | bytes 98312 | tf_op jit(solution)/shard_map/ppermute | solution.py:29
  35.2 5.3 %collective-permute-start.6 = (f32[34,1,256]{2,1,0:T(1,128)S(1)}, f32[34,1,256]{2,1,0:T(1,128)S(1)}, u32[]{:S(2)}, u32[]{:S(2)}) collective-permute-start(f32[34,1,256]{2,1,0:T(1,128)S(1)} %get-tuple-element.51), channel_id=1, source_target_pairs={{0,1},{1,2},{2,3},{3,4},{4,5},{5,6},{6,7},{7,8},{8,9},{9,10},{10,1... | collective-permute-start | bytes 104456 | tf_op jit(solution)/shard_map/ppermute | solution.py:26
  37.1 6.8 %collective-permute-start.7 = (f32[34,1,256]{2,1,0:T(1,128)S(1)}, f32[34,1,256]{2,1,0:T(1,128)S(1)}, u32[]{:S(2)}, u32[]{:S(2)}) collective-permute-start(f32[34,1,256]{2,1,0:T(1,128)S(1)} %get-tuple-element.52), channel_id=1, source_target_pairs={{1,0},{2,1},{3,2},{4,3},{5,4},{6,5},{7,6},{8,7},{9,8},{10,9},{11,1... | collective-permute-start | bytes 104456 | tf_op jit(solution)/shard_map/ppermute | solution.py:29
  50.6 5.2 %collective-permute-start.9 = (f32[1,32,256]{2,1,0:T(8,128)S(1)}, f32[1,32,256]{2,1,0:T(8,128)S(1)}, u32[]{:S(2)}, u32[]{:S(2)}) collective-permute-start(f32[1,32,256]{2,1,0:T(8,128)S(1)} %get-tuple-element.70), channel_id=1, source_target_pairs={{16,0},{32,16},{48,32},{64,48},{80,64},{96,80},{112,96},{17,1},{33... | collective-permute-start | bytes 98312 | tf_op jit(solution)/shard_map/ppermute | solution.py:29
  55.9 5.3 %collective-permute-start.10 = (f32[34,1,256]{2,1,0:T(1,128)S(1)}, f32[34,1,256]{2,1,0:T(1,128)S(1)}, u32[]{:S(2)}, u32[]{:S(2)}) collective-permute-start(f32[34,1,256]{2,1,0:T(1,128)S(1)} %get-tuple-element.49), channel_id=1, source_target_pairs={{0,1},{1,2},{2,3},{3,4},{4,5},{5,6},{6,7},{7,8},{8,9},{9,10},{10,1... | collective-permute-start | bytes 104456 | tf_op jit(solution)/shard_map/ppermute | solution.py:26
  57.8 6.8 %collective-permute-start.11 = (f32[34,1,256]{2,1,0:T(1,128)S(1)}, f32[34,1,256]{2,1,0:T(1,128)S(1)}, u32[]{:S(2)}, u32[]{:S(2)}) collective-permute-start(f32[34,1,256]{2,1,0:T(1,128)S(1)} %get-tuple-element.50), channel_id=1, source_target_pairs={{1,0},{2,1},{3,2},{4,3},{5,4},{6,5},{7,6},{8,7},{9,8},{10,9},{11,1... | collective-permute-start | bytes 104456 | tf_op jit(solution)/shard_map/ppermute | solution.py:29
  71.4 5.2 %collective-permute-start.13 = (f32[1,32,256]{2,1,0:T(8,128)S(1)}, f32[1,32,256]{2,1,0:T(8,128)S(1)}, u32[]{:S(2)}, u32[]{:S(2)}) collective-permute-start(f32[1,32,256]{2,1,0:T(8,128)S(1)} %get-tuple-element.68), channel_id=1, source_target_pairs={{16,0},{32,16},{48,32},{64,48},{80,64},{96,80},{112,96},{17,1},{33... | collective-permute-start | bytes 98312 | tf_op jit(solution)/shard_map/ppermute | solution.py:29
  76.7 5.3 %collective-permute-start.14 = (f32[34,1,256]{2,1,0:T(1,128)S(1)}, f32[34,1,256]{2,1,0:T(1,128)S(1)}, u32[]{:S(2)}, u32[]{:S(2)}) collective-permute-start(f32[34,1,256]{2,1,0:T(1,128)S(1)} %get-tuple-element.47), channel_id=1, source_target_pairs={{0,1},{1,2},{2,3},{3,4},{4,5},{5,6},{6,7},{7,8},{8,9},{9,10},{10,1... | collective-permute-start | bytes 104456 | tf_op jit(solution)/shard_map/ppermute | solution.py:26
  78.6 6.8 %collective-permute-start.15 = (f32[34,1,256]{2,1,0:T(1,128)S(1)}, f32[34,1,256]{2,1,0:T(1,128)S(1)}, u32[]{:S(2)}, u32[]{:S(2)}) collective-permute-start(f32[34,1,256]{2,1,0:T(1,128)S(1)} %get-tuple-element.48), channel_id=1, source_target_pairs={{1,0},{2,1},{3,2},{4,3},{5,4},{6,5},{7,6},{8,7},{9,8},{10,9},{11,1... | collective-permute-start | bytes 104456 | tf_op jit(solution)/shard_map/ppermute | solution.py:29
  93.5 5.2 %collective-permute-start.17 = (f32[1,32,256]{2,1,0:T(8,128)S(1)}, f32[1,32,256]{2,1,0:T(8,128)S(1)}, u32[]{:S(2)}, u32[]{:S(2)}) collective-permute-start(f32[1,32,256]{2,1,0:T(8,128)S(1)} %get-tuple-element.66), channel_id=1, source_target_pairs={{16,0},{32,16},{48,32},{64,48},{80,64},{96,80},{112,96},{17,1},{33... | collective-permute-start | bytes 98312 | tf_op jit(solution)/shard_map/ppermute | solution.py:29
  98.8 5.5 %collective-permute-start.18 = (f32[34,1,256]{2,1,0:T(1,128)S(1)}, f32[34,1,256]{2,1,0:T(1,128)S(1)}, u32[]{:S(2)}, u32[]{:S(2)}) collective-permute-start(f32[34,1,256]{2,1,0:T(1,128)S(1)} %get-tuple-element.45), channel_id=1, source_target_pairs={{0,1},{1,2},{2,3},{3,4},{4,5},{5,6},{6,7},{7,8},{8,9},{9,10},{10,1... | collective-permute-start | bytes 104456 | tf_op jit(solution)/shard_map/ppermute | solution.py:26
  100.7 6.8 %collective-permute-start.19 = (f32[34,1,256]{2,1,0:T(1,128)S(1)}, f32[34,1,256]{2,1,0:T(1,128)S(1)}, u32[]{:S(2)}, u32[]{:S(2)}) collective-permute-start(f32[34,1,256]{2,1,0:T(1,128)S(1)} %get-tuple-element.46), channel_id=1, source_target_pairs={{1,0},{2,1},{3,2},{4,3},{5,4},{6,5},{7,6},{8,7},{9,8},{10,9},{11,1... | collective-permute-start | bytes 104456 | tf_op jit(solution)/shard_map/ppermute | solution.py:29
  114.3 5.2 %collective-permute-start.21 = (f32[1,32,256]{2,1,0:T(8,128)S(1)}, f32[1,32,256]{2,1,0:T(8,128)S(1)}, u32[]{:S(2)}, u32[]{:S(2)}) collective-permute-start(f32[1,32,256]{2,1,0:T(8,128)S(1)} %get-tuple-element.64), channel_id=1, source_target_pairs={{16,0},{32,16},{48,32},{64,48},{80,64},{96,80},{112,96},{17,1},{33... | collective-permute-start | bytes 98312 | tf_op jit(solution)/shard_map/ppermute | solution.py:29
  119.5 5.3 %collective-permute-start.22 = (f32[34,1,256]{2,1,0:T(1,128)S(1)}, f32[34,1,256]{2,1,0:T(1,128)S(1)}, u32[]{:S(2)}, u32[]{:S(2)}) collective-permute-start(f32[34,1,256]{2,1,0:T(1,128)S(1)} %get-tuple-element.43), channel_id=1, source_target_pairs={{0,1},{1,2},{2,3},{3,4},{4,5},{5,6},{6,7},{7,8},{8,9},{9,10},{10,1... | collective-permute-start | bytes 104456 | tf_op jit(solution)/shard_map/ppermute | solution.py:26
  121.5 6.8 %collective-permute-start.23 = (f32[34,1,256]{2,1,0:T(1,128)S(1)}, f32[34,1,256]{2,1,0:T(1,128)S(1)}, u32[]{:S(2)}, u32[]{:S(2)}) collective-permute-start(f32[34,1,256]{2,1,0:T(1,128)S(1)} %get-tuple-element.44), channel_id=1, source_target_pairs={{1,0},{2,1},{3,2},{4,3},{5,4},{6,5},{7,6},{8,7},{9,8},{10,9},{11,1... | collective-permute-start | bytes 104456 | tf_op jit(solution)/shard_map/ppermute | solution.py:29
  135.1 5.2 %collective-permute-start.25 = (f32[1,32,256]{2,1,0:T(8,128)S(1)}, f32[1,32,256]{2,1,0:T(8,128)S(1)}, u32[]{:S(2)}, u32[]{:S(2)}) collective-permute-start(f32[1,32,256]{2,1,0:T(8,128)S(1)} %get-tuple-element.62), channel_id=1, source_target_pairs={{16,0},{32,16},{48,32},{64,48},{80,64},{96,80},{112,96},{17,1},{33... | collective-permute-start | bytes 98312 | tf_op jit(solution)/shard_map/ppermute | solution.py:29
  140.4 49.9 %collective-permute-start.26 = (f32[34,1,256]{2,1,0:T(1,128)S(1)}, f32[34,1,256]{2,1,0:T(1,128)S(1)}, u32[]{:S(2)}, u32[]{:S(2)}) collective-permute-start(f32[34,1,256]{2,1,0:T(1,128)S(1)} %get-tuple-element.41), channel_id=1, source_target_pairs={{0,1},{1,2},{2,3},{3,4},{4,5},{5,6},{6,7},{7,8},{8,9},{9,10},{10,1... | collective-permute-start | bytes 104456 | tf_op jit(solution)/shard_map/ppermute | solution.py:26
  142.3 48.0 %collective-permute-start.27 = (f32[34,1,256]{2,1,0:T(1,128)S(1)}, f32[34,1,256]{2,1,0:T(1,128)S(1)}, u32[]{:S(2)}, u32[]{:S(2)}) collective-permute-start(f32[34,1,256]{2,1,0:T(1,128)S(1)} %get-tuple-element.42), channel_id=1, source_target_pairs={{1,0},{2,1},{3,2},{4,3},{5,4},{6,5},{7,6},{8,7},{9,8},{10,9},{11,1... | collective-permute-start | bytes 104456 | tf_op jit(solution)/shard_map/ppermute | solution.py:29
  201.2 5.2 %collective-permute-start.29 = (f32[1,32,256]{2,1,0:T(8,128)S(1)}, f32[1,32,256]{2,1,0:T(8,128)S(1)}, u32[]{:S(2)}, u32[]{:S(2)}) collective-permute-start(f32[1,32,256]{2,1,0:T(8,128)S(1)} %get-tuple-element.60), channel_id=1, source_target_pairs={{16,0},{32,16},{48,32},{64,48},{80,64},{96,80},{112,96},{17,1},{33... | collective-permute-start | bytes 98312 | tf_op jit(solution)/shard_map/ppermute | solution.py:29
  206.5 7.7 %collective-permute-start.30 = (f32[34,1,256]{2,1,0:T(1,128)S(1)}, f32[34,1,256]{2,1,0:T(1,128)S(1)}, u32[]{:S(2)}, u32[]{:S(2)}) collective-permute-start(f32[34,1,256]{2,1,0:T(1,128)S(1)} %get-tuple-element.39), channel_id=1, source_target_pairs={{0,1},{1,2},{2,3},{3,4},{4,5},{5,6},{6,7},{7,8},{8,9},{9,10},{10,1... | collective-permute-start | bytes 104456 | tf_op jit(solution)/shard_map/ppermute | solution.py:26
  212.2 6.8 %collective-permute-start.31 = (f32[34,1,256]{2,1,0:T(1,128)S(1)}, f32[34,1,256]{2,1,0:T(1,128)S(1)}, u32[]{:S(2)}, u32[]{:S(2)}) collective-permute-start(f32[34,1,256]{2,1,0:T(1,128)S(1)} %get-tuple-element.40), channel_id=1, source_target_pairs={{1,0},{2,1},{3,2},{4,3},{5,4},{6,5},{7,6},{8,7},{9,8},{10,9},{11,1... | collective-permute-start | bytes 104456 | tf_op jit(solution)/shard_map/ppermute | solution.py:29
  223.5 5.3 %collective-permute-start.32 = (f32[1,32,256]{2,1,0:T(8,128)S(1)}, f32[1,32,256]{2,1,0:T(8,128)S(1)}, u32[]{:S(2)}, u32[]{:S(2)}) collective-permute-start(f32[1,32,256]{2,1,0:T(8,128)S(1)} %get-tuple-element.57), channel_id=1, source_target_pairs={{0,16},{16,32},{32,48},{48,64},{64,80},{80,96},{96,112},{1,17},{17... | collective-permute-start | bytes 98312 | tf_op jit(solution)/shard_map/ppermute | solution.py:26
  226.9 5.2 %collective-permute-start.33 = (f32[1,32,256]{2,1,0:T(8,128)S(1)}, f32[1,32,256]{2,1,0:T(8,128)S(1)}, u32[]{:S(2)}, u32[]{:S(2)}) collective-permute-start(f32[1,32,256]{2,1,0:T(8,128)S(1)} %get-tuple-element.58), channel_id=1, source_target_pairs={{16,0},{32,16},{48,32},{64,48},{80,64},{96,80},{112,96},{17,1},{33... | collective-permute-start | bytes 98312 | tf_op jit(solution)/shard_map/ppermute | solution.py:29
  232.2 54.0 %collective-permute-start.34 = (f32[34,1,256]{2,1,0:T(1,128)S(1)}, f32[34,1,256]{2,1,0:T(1,128)S(1)}, u32[]{:S(2)}, u32[]{:S(2)}) collective-permute-start(f32[34,1,256]{2,1,0:T(1,128)S(1)} %get-tuple-element.37), channel_id=1, source_target_pairs={{0,1},{1,2},{2,3},{3,4},{4,5},{5,6},{6,7},{7,8},{8,9},{9,10},{10,1... | collective-permute-start | bytes 104456 | tf_op jit(solution)/shard_map/ppermute | solution.py:26
  234.1 52.1 %collective-permute-start.35 = (f32[34,1,256]{2,1,0:T(1,128)S(1)}, f32[34,1,256]{2,1,0:T(1,128)S(1)}, u32[]{:S(2)}, u32[]{:S(2)}) collective-permute-start(f32[34,1,256]{2,1,0:T(1,128)S(1)} %get-tuple-element.38), channel_id=1, source_target_pairs={{1,0},{2,1},{3,2},{4,3},{5,4},{6,5},{7,6},{8,7},{9,8},{10,9},{11,1... | collective-permute-start | bytes 104456 | tf_op jit(solution)/shard_map/ppermute | solution.py:29
  303.5 9.7 %collective-permute-start.38 = (f32[34,1,256]{2,1,0:T(1,128)S(1)}, f32[34,1,256]{2,1,0:T(1,128)S(1)}, u32[]{:S(2)}, u32[]{:S(2)}) collective-permute-start(f32[34,1,256]{2,1,0:T(1,128)S(1)} %get-tuple-element.35), channel_id=1, source_target_pairs={{0,1},{1,2},{2,3},{3,4},{4,5},{5,6},{6,7},{7,8},{8,9},{9,10},{10,1... | collective-permute-start | bytes 104456 | tf_op jit(solution)/shard_map/ppermute | solution.py:26
  309.3 6.8 %collective-permute-start.39 = (f32[34,1,256]{2,1,0:T(1,128)S(1)}, f32[34,1,256]{2,1,0:T(1,128)S(1)}, u32[]{:S(2)}, u32[]{:S(2)}) collective-permute-start(f32[34,1,256]{2,1,0:T(1,128)S(1)} %get-tuple-element.36), channel_id=1, source_target_pairs={{1,0},{2,1},{3,2},{4,3},{5,4},{6,5},{7,6},{8,7},{9,8},{10,9},{11,1... | collective-permute-start | bytes 104456 | tf_op jit(solution)/shard_map/ppermute | solution.py:29
  (34 other events, 686.5 us)
